TPU v7x, 256 devices: a whole 4x4x8 slice. The times are simulated.
256 devices in a mesh: dp: 128 (over x, y, z_lo, core), sub: 2 (over z_hi).
Axes of the slice: x: 4, y: 4, z: 8 (z_hi: 2, z_lo: 4; z = z_hi * 4 + z_lo), core: 2. Of those that a mesh axis runs over, the one named last changes fastest.
Arguments:
- projections: float32 [49152, 128], P(('dp', 'sub')), may hold values from -6 to 6
- partner: int32 [49152], P(('dp', 'sub')), may hold values from 0 to 49151, as said below
Outputs:
- loss: float32 [], replicated
- grad_projections: float32 [49152, 128], P(('dp', 'sub'))
Inputs may be any that keep to these rules, and one draw needn't show every extreme that they name: partner pairs the views: partner[partner[i]] = i and partner[i] != i for every view.
All inputs are finite; a program needn't handle non-finite values.
Results may differ from a plain program's by a relative error of at most 0.0003.
The roundings to bfloat16 on the way count: a program that leaves them out, or rounds other values in their place, can miss the bound.
Values may be sent and summed in bfloat16 or wider, within the bound.
No kernel may reach another device: no remote copies, remote signals or barrier semaphores. Data moves between devices by JAX's collectives and lax.ppermute only.
A program may use at most 128 MiB of HBM per device.

v0:
```python
import jax
import jax.numpy as jnp
from jax import lax
from jax.sharding import Mesh
from jax.sharding import PartitionSpec as P

DP_SUB = ("dp_0", "dp_1", "dp_2", "dp_3", "sub")
TAU = 0.1
SHIFT = 10.0


def piece_ends(length, count):
    unit = 8 if length >= 8 * count else 1
    return [length // unit * k // count * unit for k in range(1, count)]


def all_blocks(value, axes, turns):
    pieces = value[None]
    for k in turns:
        pieces = lax.all_gather(pieces, axes[k], axis=0, tiled=True)
    current = [lax.axis_size(axes[k]) for k in reversed(turns)]
    pieces = pieces.reshape(*current, *value.shape)
    turned = sorted(range(len(turns)), key=lambda place: turns[len(turns) - 1 - place])
    return pieces.transpose(*turned, *range(len(turns), pieces.ndim)).reshape(-1, *value.shape)


def laid_out(pieces, dim):
    shape = list(pieces.shape[1:])
    shape[dim] *= pieces.shape[0]
    return jnp.moveaxis(pieces, 0, dim).reshape(shape)


def gather_at_once(value, axes, dim):
    numbers = list(range(len(axes)))[::-1]
    cut = value.shape.index(max(value.shape[:-1] or value.shape))
    edges = [0, *piece_ends(value.shape[cut], len(axes)), value.shape[cut]]
    gathered = []
    for k, (start, end) in enumerate(zip(edges, edges[1:])):
        if end > start:
            slab = lax.slice_in_dim(value, start, end, axis=cut)
            gathered.append(all_blocks(slab, axes, numbers[k:] + numbers[:k]))
    return laid_out(jnp.concatenate(gathered, axis=cut + 1), dim)


def by_axis(value, axes):
    for axis in axes:
        value = lax.psum(value, axis)
    return value


def tile_scores(left_low, piece):
    return (
        lax.dot_general(
            left_low, piece, (((1,), (1,)), ((), ())), preferred_element_type=jnp.float32
        )
        / TAU
    )


def local_fold(fn, init, gathered, width):
    blocks = gathered.shape[0] // width

    def step(index, carry):
        start = (index * width).astype(jnp.int32)
        piece = lax.dynamic_slice_in_dim(gathered, start, width, 0)
        return fn(carry, piece, start)

    return lax.fori_loop(0, blocks, step, init)


def make_forward(left_low, row_ids, mates, column_ids):

    def forward_step(carry, piece, start):
        total, pos = carry
        score = tile_scores(left_low, piece)
        cols = column_ids(start, piece.shape[0])
        diag = cols[None, :] == row_ids[:, None]
        hit = cols[None, :] == mates[:, None]
        total = total + jnp.sum(jnp.where(diag, 0.0, jnp.exp(score - SHIFT)), axis=1)
        pos = pos + jnp.sum(jnp.where(hit, score, 0.0), axis=1)
        return (total, pos)

    return forward_step


def make_backward(left_low, row_ids, mates, column_ids, lse_rows, lse_cols):

    def backward_step(carry, piece, start):
        score = tile_scores(left_low, piece)
        count = piece.shape[0]
        cols = column_ids(start, count)
        diag = cols[None, :] == row_ids[:, None]
        hit = cols[None, :] == mates[:, None]
        lse_piece = lax.dynamic_slice_in_dim(lse_cols, start, count, 0)
        weight = jnp.exp(score - lse_rows[:, None]) + jnp.exp(score - lse_piece[None, :])
        weight = weight - 2.0 * hit.astype(jnp.float32)
        weight = jnp.where(diag, 0.0, weight / TAU).astype(jnp.bfloat16)
        return carry + jnp.dot(weight, piece, preferred_element_type=jnp.float32)

    return backward_step


def body(projections, partner):
    vrows = projections.shape[0]
    width_d = projections.shape[1]
    groups = lax.axis_size(DP_SUB)
    views_all = vrows * groups
    inverse = lax.rsqrt(jnp.sum(projections * projections, axis=1) + 1e-06)
    unit = projections * inverse[:, None]
    unit_low = unit.astype(jnp.bfloat16)
    rows = lax.axis_index(DP_SUB) * vrows + jnp.arange(vrows, dtype=jnp.int32)

    def plain_ids(start, count):
        return start + jnp.arange(count, dtype=jnp.int32)

    forward_step = make_forward(unit_low, rows, partner, plain_ids)
    empty = jnp.zeros((vrows,), jnp.float32)
    width = vrows * 16
    gathered = gather_at_once(unit_low, DP_SUB, 0)
    total, pos = local_fold(forward_step, (empty, empty), gathered, width)
    lse = jnp.log(total) + SHIFT
    row_loss = lse - pos
    lse_all = lax.all_gather(lse, DP_SUB, axis=0, tiled=True)
    loss = by_axis(jnp.sum(row_loss), DP_SUB) / views_all
    backward_step = make_backward(unit_low, rows, partner, plain_ids, lse, lse_all)
    start_grad = jnp.zeros((vrows, width_d), jnp.float32)
    grad_unit = local_fold(backward_step, start_grad, gathered, width)
    inner = jnp.sum(unit * grad_unit, axis=1)
    grad = inverse[:, None] * (grad_unit - unit * inner[:, None])
    return (loss, grad)


def solution(mesh):
    finer = Mesh(
        mesh.devices.reshape(4, 4, 4, 2, mesh.shape["sub"]), ("dp_0", "dp_1", "dp_2", "dp_3", "sub")
    )
    in_specs = (P(DP_SUB, None), P(DP_SUB))
    out_specs = (P(), P(DP_SUB, None))
    return jax.shard_map(body, mesh=finer, in_specs=in_specs, out_specs=out_specs, check_vma=False)
```

profile of v0, /device:TPU:1, one launch (start us, length us, event | category | flops | bytes accessed | tf_op | source)
XLA Modules:
  0.0 718.0 jit_solution(9662809372564612045)
XLA Ops:
  9.2 12.2 %all-gather.2 = bf16[160,128]{1,0:T(8,128)(2,1)S(1)} all-gather(bf16[40,128]{1,0:T(8,128)(2,1)S(1)} %get-tuple-element.414), channel_id=4, replica_groups=mesh['dp_0'=4,'dp_1'=4,'dp_2'=4,'dp_3'=2,'sub'=2] {'dp_2'}, dimensions={0}, use_global_device_ids=true | all-gather | bytes 51200 | tf_op jit(solution)/shard_map/all_gather | solution.py:20
  21.4 9.7 %all_gather.89 = bf16[16,40,128]{2,1,0:T(8,128)(2,1)S(1)} all-gather(bf16[4,40,128]{2,1,0:T(8,128)(2,1)S(1)} %bitcast.53), channel_id=1, replica_groups=mesh['dp_0'=4,'dp_1'=4,'dp_2'=4,'dp_3'=2,'sub'=2] {'dp_1'}, dimensions={0}, use_global_device_ids=true | all-gather | bytes 204800 | tf_op jit(solution)/shard_map/all_gather | solution.py:20
  31.1 11.2 %all_gather.90 = bf16[64,40,128]{2,1,0:T(8,128)(2,1)} all-gather(bf16[16,40,128]{2,1,0:T(8,128)(2,1)S(1)} %all_gather.89), channel_id=1, replica_groups=mesh['dp_0'=4,'dp_1'=4,'dp_2'=4,'dp_3'=2,'sub'=2] {'dp_0'}, dimensions={0}, use_global_device_ids=true | all-gather | bytes 819200 | tf_op jit(solution)/shard_map/all_gather | solution.py:20
  42.4 10.7 %all-gather.1 = bf16[80,128]{1,0:T(8,128)(2,1)S(1)} all-gather(bf16[40,128]{1,0:T(8,128)(2,1)S(1)} %get-tuple-element.415), channel_id=3, replica_groups=mesh['dp_0'=4,'dp_1'=4,'dp_2'=4,'dp_3'=2,'sub'=2] {'dp_3'}, dimensions={0}, use_global_device_ids=true | all-gather | bytes 30720 | tf_op jit(solution)/shard_map/all_gather | solution.py:20
  53.0 10.8 %all_gather.84 = bf16[8,40,128]{2,1,0:T(8,128)(2,1)S(1)} all-gather(bf16[2,40,128]{2,1,0:T(8,128)(2,1)S(1)} %bitcast.56), channel_id=1, replica_groups=mesh['dp_0'=4,'dp_1'=4,'dp_2'=4,'dp_3'=2,'sub'=2] {'dp_2'}, dimensions={0}, use_global_device_ids=true | all-gather | bytes 102400 | tf_op jit(solution)/shard_map/all_gather | solution.py:20
  63.8 10.5 %all_gather.85 = bf16[32,40,128]{2,1,0:T(8,128)(2,1)} all-gather(bf16[8,40,128]{2,1,0:T(8,128)(2,1)S(1)} %all_gather.84), channel_id=1, replica_groups=mesh['dp_0'=4,'dp_1'=4,'dp_2'=4,'dp_3'=2,'sub'=2] {'dp_1'}, dimensions={0}, use_global_device_ids=true | all-gather | bytes 409600 | tf_op jit(solution)/shard_map/all_gather | solution.py:20
  74.4 8.3 %all-gather = bf16[64,128]{1,0:T(8,128)(2,1)S(1)} all-gather(bf16[32,128]{1,0:T(8,128)(2,1)S(1)} %slice.20), channel_id=2, replica_groups=mesh['dp_0'=4,'dp_1'=4,'dp_2'=4,'dp_3'=2,'sub'=2] {'sub'}, dimensions={0}, use_global_device_ids=true | all-gather | bytes 24576 | tf_op jit(solution)/shard_map/all_gather | solution.py:20
  82.8 7.8 %all_gather.79 = bf16[4,32,128]{2,1,0:T(8,128)(2,1)S(1)} all-gather(bf16[2,32,128]{2,1,0:T(8,128)(2,1)S(1)} %bitcast.57), channel_id=1, replica_groups=mesh['dp_0'=4,'dp_1'=4,'dp_2'=4,'dp_3'=2,'sub'=2] {'dp_3'}, dimensions={0}, use_global_device_ids=true | all-gather | bytes 49152 | tf_op jit(solution)/shard_map/all_gather | solution.py:20
  90.6 14.0 %all_gather.80 = bf16[16,32,128]{2,1,0:T(8,128)(2,1)S(1)} all-gather(bf16[4,32,128]{2,1,0:T(8,128)(2,1)S(1)} %all_gather.79), channel_id=1, replica_groups=mesh['dp_0'=4,'dp_1'=4,'dp_2'=4,'dp_3'=2,'sub'=2] {'dp_2'}, dimensions={0}, use_global_device_ids=true | all-gather | bytes 163840 | tf_op jit(solution)/shard_map/all_gather | solution.py:20
  104.6 11.5 %all_gather.81 = bf16[64,32,128]{2,1,0:T(8,128)(2,1)} all-gather(bf16[16,32,128]{2,1,0:T(8,128)(2,1)S(1)} %all_gather.80), channel_id=1, replica_groups=mesh['dp_0'=4,'dp_1'=4,'dp_2'=4,'dp_3'=2,'sub'=2] {'dp_1'}, dimensions={0}, use_global_device_ids=true | all-gather | bytes 655360 | tf_op jit(solution)/shard_map/all_gather | solution.py:20
  116.8 9.8 %all-gather.3 = bf16[160,128]{1,0:T(8,128)(2,1)S(1)} all-gather(bf16[40,128]{1,0:T(8,128)(2,1)S(1)} %get-tuple-element.413), channel_id=5, replica_groups=mesh['dp_0'=4,'dp_1'=4,'dp_2'=4,'dp_3'=2,'sub'=2] {'dp_1'}, dimensions={0}, use_global_device_ids=true | all-gather | bytes 51200 | tf_op jit(solution)/shard_map/all_gather | solution.py:20
  126.6 9.4 %all_gather.94 = bf16[16,40,128]{2,1,0:T(8,128)(2,1)S(1)} all-gather(bf16[4,40,128]{2,1,0:T(8,128)(2,1)S(1)} %bitcast.54), channel_id=1, replica_groups=mesh['dp_0'=4,'dp_1'=4,'dp_2'=4,'dp_3'=2,'sub'=2] {'dp_0'}, dimensions={0}, use_global_device_ids=true | all-gather | bytes 204800 | tf_op jit(solution)/shard_map/all_gather | solution.py:20
  136.0 10.5 %all_gather.95 = bf16[32,40,128]{2,1,0:T(8,128)(2,1)S(1)} all-gather(bf16[16,40,128]{2,1,0:T(8,128)(2,1)S(1)} %all_gather.94), channel_id=1, replica_groups=mesh['dp_0'=4,'dp_1'=4,'dp_2'=4,'dp_3'=2,'sub'=2] {'sub'}, dimensions={0}, use_global_device_ids=true | all-gather | bytes 491520 | tf_op jit(solution)/shard_map/all_gather | solution.py:20
  146.5 12.8 %all_gather.96 = bf16[64,40,128]{2,1,0:T(8,128)(2,1)} all-gather(bf16[32,40,128]{2,1,0:T(8,128)(2,1)S(1)} %all_gather.95), channel_id=1, replica_groups=mesh['dp_0'=4,'dp_1'=4,'dp_2'=4,'dp_3'=2,'sub'=2] {'dp_3'}, dimensions={0}, use_global_device_ids=true | all-gather | bytes 983040 | tf_op jit(solution)/shard_map/all_gather | solution.py:20
  159.4 9.2 %all-gather.4 = bf16[160,128]{1,0:T(8,128)(2,1)S(1)} all-gather(bf16[40,128]{1,0:T(8,128)(2,1)S(1)} %get-tuple-element.412), channel_id=6, replica_groups=mesh['dp_0'=4,'dp_1'=4,'dp_2'=4,'dp_3'=2,'sub'=2] {'dp_0'}, dimensions={0}, use_global_device_ids=true | all-gather | bytes 51200 | tf_op jit(solution)/shard_map/all_gather | solution.py:20
  168.6 7.5 %all_gather.99 = bf16[8,40,128]{2,1,0:T(8,128)(2,1)S(1)} all-gather(bf16[4,40,128]{2,1,0:T(8,128)(2,1)S(1)} %bitcast.55), channel_id=1, replica_groups=mesh['dp_0'=4,'dp_1'=4,'dp_2'=4,'dp_3'=2,'sub'=2] {'sub'}, dimensions={0}, use_global_device_ids=true | all-gather | bytes 122880 | tf_op jit(solution)/shard_map/all_gather | solution.py:20
  176.1 5.7 all_gather.100
  181.8 15.9 %all_gather.101 = bf16[64,40,128]{2,1,0:T(8,128)(2,1)} all-gather(bf16[16,40,128]{2,1,0:T(8,128)(2,1)S(1)} %all_gather.100), channel_id=1, replica_groups=mesh['dp_0'=4,'dp_1'=4,'dp_2'=4,'dp_3'=2,'sub'=2] {'dp_2'}, dimensions={0}, use_global_device_ids=true | all-gather | bytes 819200 | tf_op jit(solution)/shard_map/all_gather | solution.py:20
  198.6 3.5 constant_dynamic-update-slice_fusion.4
  204.5 37.0 %all-gather.23.cloned.1.call-done = bf16[256,40,128]{2,1,0:T(8,128)(2,1)} async-done(((bf16[64,40,128]{2,1,0:T(8,128)(2,1)}), bf16[256,40,128]{2,1,0:T(8,128)(2,1)}) %all-gather.23.cloned.1.call-update) | async-done | bytes 2621456 | tf_op jit(solution)/shard_map/all_gather | solution.py:20
  241.5 3.9 copy.10
  245.4 35.6 %all-gather.25.cloned.1.call-done = bf16[256,40,128]{2,1,0:T(8,128)(2,1)} async-done(((bf16[64,40,128]{2,1,0:T(8,128)(2,1)}), bf16[256,40,128]{2,1,0:T(8,128)(2,1)}) %all-gather.25.cloned.1.call-update) | async-done | bytes 2621456 | tf_op jit(solution)/shard_map/all_gather | solution.py:20
  280.9 3.9 copy.11
  284.8 74.8 %all-gather.17.cloned.1.call-done = bf16[256,40,128]{2,1,0:T(8,128)(2,1)} async-done(((bf16[128,40,128]{2,1,0:T(8,128)(2,1)}), bf16[256,40,128]{2,1,0:T(8,128)(2,1)}) %all-gather.17.cloned.1.call-update) | async-done | bytes 2621456 | tf_op jit(solution)/shard_map/all_gather | solution.py:20
  371.1 35.9 %while.32 = (s32[]{:T(128)}, f32[192]{0:T(256)S(1)}, f32[192]{0:T(256)S(1)}, bf16[49152,128]{1,0:T(8,128)(2,1)}, bf16[192,128]{1,0:T(8,128)(2,1)S(1)}, /*index=5...) while((s32[]{:T(128)}, f32[192]{0:T(256)S(1)}, ...), condition=%wide.region_4.5_spmd.clone, body=%wide.region_1.4_spmd.clone.sunk | while | flops 155717184 | bytes 868785 | solution.py:68
  408.5 9.1 %psum.35 = f32[]{:T(128)} all-reduce(f32[]{:T(128)} %get-tuple-element.417), channel_id=1, replica_groups=mesh['dp_0'=4,'dp_1'=4,'dp_2'=4,'dp_3'=2,'sub'=2] {'dp_0'}, use_global_device_ids=true, to_apply=%region_6.7 | all-reduce | flops 1 | bytes 8 | tf_op jit(solution)/shard_map/psum | solution.py:47
  417.6 9.4 %psum.36 = f32[]{:T(128)} all-reduce(f32[]{:T(128)} %psum.35), channel_id=1, replica_groups=mesh['dp_0'=4,'dp_1'=4,'dp_2'=4,'dp_3'=2,'sub'=2] {'dp_1'}, use_global_device_ids=true, to_apply=%region_7.8 | all-reduce | flops 1 | bytes 8 | tf_op jit(solution)/shard_map/psum | solution.py:47
  427.0 7.5 %psum.37 = f32[]{:T(128)} all-reduce(f32[]{:T(128)} %psum.36), channel_id=1, replica_groups=mesh['dp_0'=4,'dp_1'=4,'dp_2'=4,'dp_3'=2,'sub'=2] {'dp_2'}, use_global_device_ids=true, to_apply=%region_8.9 | all-reduce | flops 1 | bytes 8 | tf_op jit(solution)/shard_map/psum | solution.py:47
  434.5 8.8 %psum.38 = f32[]{:T(128)} all-reduce(f32[]{:T(128)} %psum.37), channel_id=1, replica_groups=mesh['dp_0'=4,'dp_1'=4,'dp_2'=4,'dp_3'=2,'sub'=2] {'dp_3'}, use_global_device_ids=true, to_apply=%region_9.10 | all-reduce | flops 1 | bytes 8 | tf_op jit(solution)/shard_map/psum | solution.py:47
  443.4 8.3 %psum.39 = f32[]{:T(128)} all-reduce(f32[]{:T(128)} %psum.38), channel_id=1, replica_groups=mesh['dp_0'=4,'dp_1'=4,'dp_2'=4,'dp_3'=2,'sub'=2] {'sub'}, use_global_device_ids=true, to_apply=%region_10.11 | all-reduce | flops 1 | bytes 8 | tf_op jit(solution)/shard_map/psum | solution.py:47
  452.3 198.8 %all-reduce.3.cloned.1.call-done = f32[49152]{0:T(1024)} async-done(((f32[49152]{0:T(1024)}), f32[49152]{0:T(1024)}) %all-reduce.3.cloned.1.call-update) | async-done | bytes 196624
  651.2 57.9 %while.33 = (s32[]{:T(128)}, f32[192,128]{1,0:T(8,128)S(1)}, bf16[49152,128]{1,0:T(8,128)(2,1)}, bf16[192,128]{1,0:T(8,128)(2,1)S(1)}, f32[192]{0:T(256)S(1)}, /...) while((s32[]{:T(128)}, f32[192,128]{1,0:T(8,128)S(1)}, ...), condition=%wide.region_12.13_spmd.clone, body=%wide.region_11.12_spmd.clone.sunk | while | flops 308530368 | bytes 1884856 | solution.py:68
  (176 shorter events, 112.6 us)
Async XLA Ops:
  7.2 109.0 %all-gather.19.cloned.1.call-start = ((), (), s32[]{:S(2)}) async-start(), calls=%async_computation.3 | async-start | bytes 1966080 | tf_op jit(solution)/shard_map/all_gather | solution.py:20
  42.3 155.5 %all-gather.15.cloned.1.call-start = ((), (), s32[]{:S(2)}) async-start(), calls=%async_computation.1 | async-start | bytes 1638400 | tf_op jit(solution)/shard_map/all_gather | solution.py:20
  74.4 124.2 %all-gather.13.cloned.1.call-start = ((), (), s32[]{:S(2)}) async-start(), calls=%async_computation | async-start | bytes 2621440 | tf_op jit(solution)/shard_map/all_gather | solution.py:20
  116.1 86.0 %all-gather.21.cloned.1.call-start = ((), (), s32[]{:S(2)}) async-start(), calls=%async_computation.4 | async-start | bytes 3932160 | tf_op jit(solution)/shard_map/all_gather | solution.py:20
  116.7 124.8 %all-gather.23.cloned.1.call-start = ((), (), s32[]{:S(2)}) async-start(), calls=%async_computation.5 | async-start | bytes 3276800 | tf_op jit(solution)/shard_map/all_gather | solution.py:20
  159.4 121.6 %all-gather.25.cloned.1.call-start = ((), (), s32[]{:S(2)}) async-start(), calls=%async_computation.6 | async-start | bytes 3276800 | tf_op jit(solution)/shard_map/all_gather | solution.py:20
  197.7 161.9 %all-gather.17.cloned.1.call-start = ((), (), s32[]{:S(2)}) async-start(), calls=%async_computation.2 | async-start | bytes 3932160 | tf_op jit(solution)/shard_map/all_gather | solution.py:20
  198.5 452.7 %all-reduce.3.cloned.1.call-start = ((), (), s32[]{:S(2)}) async-start(), calls=%async_computation.7 | async-start | bytes 393216
  364.0 2.5 copy-start
  366.5 2.5 copy-start.1
  369.0 2.1 copy-start.4
  407.8 0.7 copy-start.3
  651.2 57.9 %copy-start.2 = (f32[192,128]{1,0:T(8,128)S(1)}, f32[192,128]{1,0:T(8,128)}, u32[]{:S(2)}) copy-start(f32[192,128]{1,0:T(8,128)} %param.6) | copy-start | bytes 294916
Sparse Core Ops, SparseCore 0:
  42.5 57.3 all-gather.18
  101.6 22.8 all-gather.14
  126.4 35.5 all-gather.12
  163.6 17.1 all-gather.20
  182.5 58.9 all-gather.22
  243.1 37.7 all-gather.24
  282.7 76.8 all-gather.16
  408.7 242.4 all-reduce.2
where the time goes:
time: 721 us; the launch traced here: 718 us
  waiting for transfers between devices  348 us (48%)
  blocking collectives  231 us (32%)
  matrix products  80.8 us (11%)
  local copies, waits for them, and re-layouts  37.3 us (5%)
  between operations  16.1 us (2%)
    unnamed x9, waiting for transfers between devices  200 us
    all_gather x18, blocking collectives, all_blocks(): pieces = lax.all_gather(pieces, axes[k], axis=0, tiled=True)  188 us
    all_gather x7, waiting for transfers between devices, all_blocks(): pieces = lax.all_gather(pieces, axes[k], axis=0, tiled=True)  147 us
    dot_general x16, matrix products, backward_step(): return carry + jnp.dot(weight, piece, preferred_element_type=jnp.float32)  45.9 us
    psum x5, blocking collectives, by_axis(): value = lax.psum(value, axis)  43.2 us
    dot_general x16, matrix products, tile_scores(): lax.dot_general(left_low, piece, (((1,), (1,)), ((), ())), preferred_elem...  34.9 us
  transfers between devices with their start and end apart: 8, of which 4 were waited for; matrix products, arithmetic and copies ran while one was open for 2% of the time, Pallas kernels for 0%

commit v1 on v0

--- a/solution.py
+++ b/solution.py
@@ -17,7 +17,9 @@
 def all_blocks(value, axes, turns):
     pieces = value[None]
     for k in turns:
-        pieces = lax.all_gather(pieces, axes[k], axis=0, tiled=True)
+        pieces = jnp.concatenate(
+            lax.all_to_all(jnp.stack([pieces] * lax.axis_size(axes[k])), axes[k], 0, 0), axis=0
+        )
     current = [lax.axis_size(axes[k]) for k in reversed(turns)]
     pieces = pieces.reshape(*current, *value.shape)
     turned = sorted(range(len(turns)), key=lambda place: turns[len(turns) - 1 - place])

time: 721 us -> 808 us (1.12)
  starting transfers between devices: 0.32 us -> 46.2 us
  blocking collectives: 231 us -> 274 us
  waiting for transfers between devices: 348 us -> 335 us
    all_to_all x0 -> x15, blocking collectives: none -> 232 us  [all_blocks(): lax.all_to_all(jnp.stack([pieces] * lax.axis_size(axes[k])), axes[k], 0, 0)]
    all_gather x18 -> x0, blocking collectives: 188 us -> none  [all_blocks(): pieces = lax.all_gather(pieces, axes[k], axis=0, tiled=True)]
    all_gather x7 -> x0, waiting for transfers between devices: 147 us -> none  [all_blocks(): pieces = lax.all_gather(pieces, axes[k], axis=0, tiled=True)]
    all_to_all x0 -> x10, waiting for transfers between devices: none -> 132 us  [all_blocks(): lax.all_to_all(jnp.stack([pieces] * lax.axis_size(axes[k])), axes[k], 0, 0)]
    all_to_all x0 -> x10, starting transfers between devices: none -> 46.1 us  [all_blocks(): lax.all_to_all(jnp.stack([pieces] * lax.axis_size(axes[k])), axes[k], 0, 0)]
    another operation x0 -> x17, local copies, waits for them, and re-layouts: none -> 11.5 us  [the longest x16 11.1 us: all_blocks(): jnp.stack([pieces] * lax.axis_size(axes[k]))]
    unnamed x9 -> x2, waiting for transfers between devices: 200 us -> 202 us
  transfers between devices with their start and end apart: 8 -> 11, of which waited for: 4 -> 11; matrix products, arithmetic and copies ran while one was open for 2% -> 2% of each run, Pallas kernels for 0% -> 0%
where the time goes in v1:
time: 808 us; the launch traced here: 804 us
  waiting for transfers between devices  335 us (41%)
  blocking collectives  274 us (34%)
  matrix products  80.6 us (10%)
  starting transfers between devices  46.2 us (6%)
  local copies, waits for them, and re-layouts  40.5 us (5%)
  between operations  16.1 us (2%)
  other arithmetic  10.9 us (1%)
    all_to_all x15, blocking collectives, all_blocks(): lax.all_to_all(jnp.stack([pieces] * lax.axis_size(axes[k])), axes[k], 0, 0)  232 us
    unnamed x2, waiting for transfers between devices  202 us
    all_to_all x10, waiting for transfers between devices, all_blocks(): lax.all_to_all(jnp.stack([pieces] * lax.axis_size(axes[k])), axes[k], 0, 0)  132 us
    all_to_all x10, starting transfers between devices, all_blocks(): lax.all_to_all(jnp.stack([pieces] * lax.axis_size(axes[k])), axes[k], 0, 0)  46.1 us
    dot_general x16, matrix products, backward_step(): return carry + jnp.dot(weight, piece, preferred_element_type=jnp.float32)  45.7 us
    psum x5, blocking collectives, by_axis(): value = lax.psum(value, axis)  41.9 us
    dot_general x16, matrix products, tile_scores(): lax.dot_general(left_low, piece, (((1,), (1,)), ((), ())), preferred_elem...  34.9 us
  transfers between devices with their start and end apart: 11, of which 11 were waited for; matrix products, arithmetic and copies ran while one was open for 2% of the time, Pallas kernels for 0%

profile of v1, /device:TPU:1, one launch (start us, length us, event | category | flops | bytes accessed | tf_op | source)
XLA Modules:
  0.0 803.8 jit_solution(14785842687901277033)
XLA Ops:
  9.8 9.0 %all-to-all-start = ((bf16[2,1,32,128]{3,2,1,0:T(8,128)(2,1)}), bf16[2,1,32,128]{3,2,1,0:T(8,128)(2,1)S(1)}, u32[]{:S(2)}, u32[]{:S(2)}) async-start(bf16[2,1,32,128]{3,2,1,0:T(8,128)(2,1)} %pad_maximum_fusion.9), calls=%async_computation | async-start | bytes 32768 | tf_op jit(solution)/shard_map/all_to_all | solution.py:21
  19.4 6.1 all-to-all-done
  25.5 5.3 all-to-all-start.5
  35.5 8.1 %all_to_all.126 = bf16[4,1,40,128]{3,2,1,0:T(8,128)(2,1)S(1)} all-to-all(bf16[4,1,40,128]{3,2,1,0:T(8,128)(2,1)S(1)} %stack.95), channel_id=1, replica_groups=mesh['dp_0'=4,'dp_1'=4,'dp_2'=4,'dp_3'=2,'sub'=2] {'dp_0'}, dimensions={0} | all-to-all | bytes 81920 | tf_op jit(solution)/shard_map/all_to_all | solution.py:21
  52.8 9.3 %all_to_all.127 = bf16[2,4,40,128]{3,2,1,0:T(8,128)(2,1)S(1)} all-to-all(bf16[2,4,40,128]{3,2,1,0:T(8,128)(2,1)S(1)} %pad_maximum_fusion.6), channel_id=1, replica_groups=mesh['dp_0'=4,'dp_1'=4,'dp_2'=4,'dp_3'=2,'sub'=2] {'sub'}, dimensions={0} | all-to-all | bytes 163840 | tf_op jit(solution)/shard_map/all_to_all | solution.py:21
  70.5 9.0 %all_to_all.128 = bf16[2,8,40,128]{3,2,1,0:T(8,128)(2,1)S(1)} all-to-all(bf16[2,8,40,128]{3,2,1,0:T(8,128)(2,1)S(1)} %pad_maximum_fusion.5), channel_id=1, replica_groups=mesh['dp_0'=4,'dp_1'=4,'dp_2'=4,'dp_3'=2,'sub'=2] {'dp_3'}, dimensions={0} | all-to-all | bytes 327680 | tf_op jit(solution)/shard_map/all_to_all | solution.py:21
  79.5 7.1 all_to_all.129
  86.7 7.4 all_to_all.130
  94.0 7.4 all_to_all.131
  105.4 4.7 all-to-all-done.2
  110.1 10.9 %all_to_all.132 = bf16[2,16,40,128]{3,2,1,0:T(8,128)(2,1)S(1)} all-to-all(bf16[2,16,40,128]{3,2,1,0:T(8,128)(2,1)S(1)} %pad_maximum_fusion.4), channel_id=1, replica_groups=mesh['dp_0'=4,'dp_1'=4,'dp_2'=4,'dp_3'=2,'sub'=2] {'sub'}, dimensions={0} | all-to-all | bytes 655360 | tf_op jit(solution)/shard_map/all_to_all | solution.py:21
  125.3 5.8 all-to-all-done.7
  131.1 11.0 %all_to_all.133 = bf16[2,32,40,128]{3,2,1,0:T(8,128)(2,1)S(1)} all-to-all(bf16[2,32,40,128]{3,2,1,0:T(8,128)(2,1)S(1)} %pad_maximum_fusion.3), channel_id=1, replica_groups=mesh['dp_0'=4,'dp_1'=4,'dp_2'=4,'dp_3'=2,'sub'=2] {'dp_3'}, dimensions={0} | all-to-all | bytes 1310720 | tf_op jit(solution)/shard_map/all_to_all | solution.py:21
  142.2 12.3 %all_to_all.134 = bf16[4,16,32,128]{3,2,1,0:T(8,128)(2,1)} all-to-all(bf16[4,16,32,128]{3,2,1,0:T(8,128)(2,1)S(1)} %stack.78), channel_id=1, replica_groups=mesh['dp_0'=4,'dp_1'=4,'dp_2'=4,'dp_3'=2,'sub'=2] {'dp_1'}, dimensions={0} | all-to-all | bytes 1048576 | tf_op jit(solution)/shard_map/all_to_all | solution.py:21
  154.6 12.1 %all_to_all.135 = bf16[4,16,40,128]{3,2,1,0:T(8,128)(2,1)S(1)} all-to-all(bf16[4,16,40,128]{3,2,1,0:T(8,128)(2,1)S(1)} %stack.87), channel_id=1, replica_groups=mesh['dp_0'=4,'dp_1'=4,'dp_2'=4,'dp_3'=2,'sub'=2] {'dp_0'}, dimensions={0} | all-to-all | bytes 1310720 | tf_op jit(solution)/shard_map/all_to_all | solution.py:21
  171.9 16.7 %all-to-all-done.23 = bf16[4,16,40,128]{3,2,1,0:T(8,128)(2,1)} async-done(((bf16[4,16,40,128]{3,2,1,0:T(8,128)(2,1)}), bf16[4,16,40,128]{3,2,1,0:T(8,128)(2,1)}, u32[]{:S(2)}, u32[]{:S(2)}) %all-to-all-start.23) | async-done | bytes 655392 | tf_op jit(solution)/shard_map/all_to_all | solution.py:21
  188.7 32.7 %all_to_all.136 = bf16[2,64,40,128]{3,2,1,0:T(8,128)(2,1)S(1)} all-to-all(bf16[2,64,40,128]{3,2,1,0:T(8,128)(2,1)S(1)} %pad_maximum_fusion.2), channel_id=1, replica_groups=mesh['dp_0'=4,'dp_1'=4,'dp_2'=4,'dp_3'=2,'sub'=2] {'sub'}, dimensions={0} | all-to-all | bytes 2621440 | tf_op jit(solution)/shard_map/all_to_all | solution.py:21
  229.6 13.8 %all-to-all-done.8 = bf16[4,32,40,128]{3,2,1,0:T(8,128)(2,1)} async-done(((bf16[4,32,40,128]{3,2,1,0:T(8,128)(2,1)}), bf16[4,32,40,128]{3,2,1,0:T(8,128)(2,1)}, u32[]{:S(2)}, u32[]{:S(2)}) %all-to-all-start.8) | async-done | bytes 1310752 | tf_op jit(solution)/shard_map/all_to_all | solution.py:21
  243.5 10.2 %all_to_all.137 = bf16[2,128,40,128]{3,2,1,0:T(8,128)(2,1)S(1)} all-to-all(bf16[2,128,40,128]{3,2,1,0:T(8,128)(2,1)} %pad_maximum_fusion.1), channel_id=1, replica_groups=mesh['dp_0'=4,'dp_1'=4,'dp_2'=4,'dp_3'=2,'sub'=2] {'dp_3'}, dimensions={0} | all-to-all | bytes 5242880 | tf_op jit(solution)/shard_map/all_to_all | solution.py:21
  254.0 29.3 %all_to_all.138 = bf16[4,64,32,128]{3,2,1,0:T(8,128)(2,1)} all-to-all(bf16[4,64,32,128]{3,2,1,0:T(8,128)(2,1)S(1)} %stack.79), channel_id=1, replica_groups=mesh['dp_0'=4,'dp_1'=4,'dp_2'=4,'dp_3'=2,'sub'=2] {'dp_0'}, dimensions={0} | all-to-all | bytes 4194304 | tf_op jit(solution)/shard_map/all_to_all | solution.py:21
  294.4 27.3 %all-to-all-done.24 = bf16[4,64,40,128]{3,2,1,0:T(8,128)(2,1)} async-done(((bf16[4,64,40,128]{3,2,1,0:T(8,128)(2,1)}), bf16[4,64,40,128]{3,2,1,0:T(8,128)(2,1)}, u32[]{:S(2)}, u32[]{:S(2)}) %all-to-all-start.24) | async-done | bytes 2621472 | tf_op jit(solution)/shard_map/all_to_all | solution.py:21
  321.7 61.4 %all_to_all.139 = bf16[2,128,40,128]{3,2,1,0:T(8,128)(2,1)} all-to-all(bf16[2,128,40,128]{3,2,1,0:T(8,128)(2,1)} %pad_maximum_fusion), channel_id=1, replica_groups=mesh['dp_0'=4,'dp_1'=4,'dp_2'=4,'dp_3'=2,'sub'=2] {'sub'}, dimensions={0} | all-to-all | bytes 5242880 | tf_op jit(solution)/shard_map/all_to_all | solution.py:21
  384.9 4.6 all-to-all-start.19
  400.2 48.2 %all-to-all-done.19 = bf16[4,64,40,128]{3,2,1,0:T(8,128)(2,1)} async-done(((bf16[4,64,40,128]{3,2,1,0:T(8,128)(2,1)}), bf16[4,64,40,128]{3,2,1,0:T(8,128)(2,1)}, u32[]{:S(2)}, u32[]{:S(2)}) %all-to-all-start.19) | async-done | bytes 2621472 | tf_op jit(solution)/shard_map/all_to_all | solution.py:21
  455.1 35.9 %while.32 = (s32[]{:T(128)}, f32[192]{0:T(256)S(1)}, f32[192]{0:T(256)S(1)}, bf16[49152,128]{1,0:T(8,128)(2,1)}, bf16[192,128]{1,0:T(8,128)(2,1)S(1)}, /*index=5...) while((s32[]{:T(128)}, f32[192]{0:T(256)S(1)}, ...), condition=%wide.region_4.5_spmd.clone, body=%wide.region_1.4_spmd.clone.sunk | while | flops 155717184 | bytes 868785 | solution.py:70
  492.5 7.8 psum.35
  500.3 7.5 psum.36
  507.8 7.3 psum.37
  515.1 11.0 %psum.38 = f32[]{:T(128)} all-reduce(f32[]{:T(128)} %psum.37), channel_id=1, replica_groups=mesh['dp_0'=4,'dp_1'=4,'dp_2'=4,'dp_3'=2,'sub'=2] {'dp_3'}, use_global_device_ids=true, to_apply=%region_9.10 | all-reduce | flops 1 | bytes 8 | tf_op jit(solution)/shard_map/psum | solution.py:49
  526.1 8.3 %psum.39 = f32[]{:T(128)} all-reduce(f32[]{:T(128)} %psum.38), channel_id=1, replica_groups=mesh['dp_0'=4,'dp_1'=4,'dp_2'=4,'dp_3'=2,'sub'=2] {'sub'}, use_global_device_ids=true, to_apply=%region_10.11 | all-reduce | flops 1 | bytes 8 | tf_op jit(solution)/shard_map/psum | solution.py:49
  535.1 202.1 %all-reduce.3.cloned.1.call-done = f32[49152]{0:T(1024)} async-done(((f32[49152]{0:T(1024)}), f32[49152]{0:T(1024)}) %all-reduce.3.cloned.1.call-update) | async-done | bytes 196624
  737.2 57.7 %while.33 = (s32[]{:T(128)}, f32[192,128]{1,0:T(8,128)S(1)}, bf16[49152,128]{1,0:T(8,128)(2,1)}, bf16[192,128]{1,0:T(8,128)(2,1)S(1)}, f32[192]{0:T(256)S(1)}, /...) while((s32[]{:T(128)}, f32[192,128]{1,0:T(8,128)S(1)}, ...), condition=%wide.region_12.13_spmd.clone, body=%wide.region_11.12_spmd.clone.sunk | while | flops 308530368 | bytes 1884856 | solution.py:70
  (201 shorter events, 172.9 us)
Async XLA Ops:
  9.8 15.7 %all-to-all-start = ((bf16[2,1,32,128]{3,2,1,0:T(8,128)(2,1)}), bf16[2,1,32,128]{3,2,1,0:T(8,128)(2,1)S(1)}, u32[]{:S(2)}, u32[]{:S(2)}) async-start(bf16[2,1,32,128]{3,2,1,0:T(8,128)(2,1)} %pad_maximum_fusion.9), calls=%async_computation | async-start | bytes 32768 | tf_op jit(solution)/shard_map/all_to_all | solution.py:21
  25.5 6.3 all-to-all-start.5
  44.3 8.5 %all-to-all-start.15 = ((bf16[4,1,40,128]{3,2,1,0:T(8,128)(2,1)}), bf16[4,1,40,128]{3,2,1,0:T(8,128)(2,1)S(1)}, u32[]{:S(2)}, u32[]{:S(2)}) async-start(bf16[4,1,40,128]{3,2,1,0:T(8,128)(2,1)} %stack.90), calls=%async_computation.15 | async-start | bytes 81920 | tf_op jit(solution)/shard_map/all_to_all | solution.py:21
  62.7 7.8 all-to-all-start.10
  102.1 8.1 %all-to-all-start.2 = ((bf16[4,4,32,128]{3,2,1,0:T(8,128)(2,1)}), bf16[4,4,32,128]{3,2,1,0:T(8,128)(2,1)S(1)}, u32[]{:S(2)}, u32[]{:S(2)}) async-start(bf16[4,4,32,128]{3,2,1,0:T(8,128)(2,1)} %stack.77), calls=%async_computation.2 | async-start | bytes 262144 | tf_op jit(solution)/shard_map/all_to_all | solution.py:21
  121.8 9.3 %all-to-all-start.7 = ((bf16[4,8,40,128]{3,2,1,0:T(8,128)(2,1)}), bf16[4,8,40,128]{3,2,1,0:T(8,128)(2,1)S(1)}, u32[]{:S(2)}, u32[]{:S(2)}) async-start(bf16[4,8,40,128]{3,2,1,0:T(8,128)(2,1)} %stack.82), calls=%async_computation.7 | async-start | bytes 655360 | tf_op jit(solution)/shard_map/all_to_all | solution.py:21
  131.1 35.6 %copy-start.4 = (bf16[4,8,40,128]{3,2,1,0:T(8,128)(2,1)}, bf16[4,8,40,128]{3,2,1,0:T(8,128)(2,1)S(1)}, u32[]{:S(2)}) copy-start(bf16[4,8,40,128]{3,2,1,0:T(8,128)(2,1)S(1)} %all-to-all-done.7) | copy-start | bytes 983044
  167.6 21.0 %all-to-all-start.23 = ((bf16[4,16,40,128]{3,2,1,0:T(8,128)(2,1)}), bf16[4,16,40,128]{3,2,1,0:T(8,128)(2,1)}, u32[]{:S(2)}, u32[]{:S(2)}) async-start(bf16[4,16,40,128]{3,2,1,0:T(8,128)(2,1)} %stack.98), calls=%async_computation.23 | async-start | bytes 1310720 | tf_op jit(solution)/shard_map/all_to_all | solution.py:21
  223.6 19.9 %all-to-all-start.8 = ((bf16[4,32,40,128]{3,2,1,0:T(8,128)(2,1)}), bf16[4,32,40,128]{3,2,1,0:T(8,128)(2,1)}, u32[]{:S(2)}, u32[]{:S(2)}) async-start(bf16[4,32,40,128]{3,2,1,0:T(8,128)(2,1)} %stack.83), calls=%async_computation.8 | async-start | bytes 2621440 | tf_op jit(solution)/shard_map/all_to_all | solution.py:21
  243.5 10.2 %copy-start.2 = (bf16[4,16,32,128]{3,2,1,0:T(8,128)(2,1)S(1)}, bf16[4,16,32,128]{3,2,1,0:T(8,128)(2,1)}, u32[]{:S(2)}) copy-start(bf16[4,16,32,128]{3,2,1,0:T(8,128)(2,1)} %all_to_all.134) | copy-start | bytes 1572868
  286.3 35.4 %all-to-all-start.24 = ((bf16[4,64,40,128]{3,2,1,0:T(8,128)(2,1)}), bf16[4,64,40,128]{3,2,1,0:T(8,128)(2,1)}, u32[]{:S(2)}, u32[]{:S(2)}) async-start(bf16[4,64,40,128]{3,2,1,0:T(8,128)(2,1)} %stack.99), calls=%async_computation.24 | async-start | bytes 5242880 | tf_op jit(solution)/shard_map/all_to_all | solution.py:21
  384.9 63.6 %all-to-all-start.19 = ((bf16[4,64,40,128]{3,2,1,0:T(8,128)(2,1)}), bf16[4,64,40,128]{3,2,1,0:T(8,128)(2,1)}, u32[]{:S(2)}, u32[]{:S(2)}) async-start(bf16[4,64,40,128]{3,2,1,0:T(8,128)(2,1)} %stack.94), calls=%async_computation.19 | async-start | bytes 5242880 | tf_op jit(solution)/shard_map/all_to_all | solution.py:21
  389.4 347.7 %all-reduce.3.cloned.1.call-start = ((), (), s32[]{:S(2)}) async-start(), calls=%async_computation.25 | async-start | bytes 393216
  389.5 1.6 copy-start.1
  392.9 2.6 copy-start
  453.0 2.2 copy-start.6
  491.8 0.7 copy-start.5
  737.2 57.7 %copy-start.3 = (f32[192,128]{1,0:T(8,128)S(1)}, f32[192,128]{1,0:T(8,128)}, u32[]{:S(2)}) copy-start(f32[192,128]{1,0:T(8,128)} %param.6) | copy-start | bytes 294916
Sparse Core Ops, SparseCore 0:
  492.6 244.4 all-reduce.2
